TPU v7x, 32 devices: a whole 2x2x4 slice. The times are simulated.
32 devices in a mesh: dp: 4 (over x, core), fsdp: 8 (over z, y).
Axes of the slice: x: 2, y: 2, z: 4, core: 2. Of those that a mesh axis runs over, the one named last changes fastest.
Arguments:
- tokens: bfloat16 [16384, 768], P(('dp', 'fsdp')), may hold values from -6 to 6
- seg_ids: int32 [16384], P(('dp', 'fsdp')), may hold values from 0 to 63, never falling along the last dimension, each value on 1 to 1024 neighbouring positions
- out_grad: bfloat16 [16384, 768], P(('dp', 'fsdp')), may hold values from -6 to 6
- first_gain: bfloat16 [768], P('fsdp'), may hold values from 0.5 to 1.5
- first_bias: bfloat16 [768], P('fsdp'), may hold values from -1.75 to 1.75
- second_gain: bfloat16 [768], P('fsdp'), may hold values from 0.5 to 1.5
- second_bias: bfloat16 [768], P('fsdp'), may hold values from -1.75 to 1.75
- qkv_weight: bfloat16 [768, 2304], P('fsdp'), may hold values from -0.21875 to 0.21875
- qkv_bias: bfloat16 [2304], P('fsdp'), may hold values from -1.75 to 1.75
- dense_weight: bfloat16 [768, 768], P('fsdp'), may hold values from -1.25 to 1.25
- up_weight: bfloat16 [768, 3072], P('fsdp'), may hold values from -0.21875 to 0.21875
- up_bias: bfloat16 [3072], P('fsdp'), may hold values from -1.75 to 1.75
- down_weight: bfloat16 [3072, 768], P('fsdp'), may hold values from -0.109375 to 0.109375
- out_bias: bfloat16 [768], P('fsdp'), may hold values from -1.75 to 1.75
Outputs:
- output: bfloat16 [16384, 768], P(('dp', 'fsdp'))
- input_grad: bfloat16 [16384, 768], P(('dp', 'fsdp'))
- first_gain_grad: float32 [768], P('fsdp')
- first_bias_grad: float32 [768], P('fsdp')
- second_gain_grad: float32 [768], P('fsdp')
- second_bias_grad: float32 [768], P('fsdp')
- qkv_weight_grad: float32 [768, 2304], P('fsdp')
- qkv_bias_grad: float32 [2304], P('fsdp')
- dense_weight_grad: float32 [768, 768], P('fsdp')
- up_weight_grad: float32 [768, 3072], P('fsdp')
- up_bias_grad: float32 [3072], P('fsdp')
- down_weight_grad: float32 [3072, 768], P('fsdp')
- out_bias_grad: float32 [768], P('fsdp')
- doc_norms: float32 [64], replicated
Inputs may be any that keep to these rules, and one draw needn't show every extreme that they name: seg_ids never falls along the stream; each document has 1 to 1024 tokens, one exactly 1024; every number below 64 occurs.
All inputs are finite; a program needn't handle non-finite values.
Results may differ from a plain program's by a relative error of at most 0.0093.
Values may be sent and summed in bfloat16 or wider, within the bound.
A program may use at most 128 MiB of HBM per device.

v0:
```python
import math

import jax
import jax.numpy as jnp
from jax import lax
from jax.sharding import PartitionSpec as P

D = 768
H = 12
HD = 64
FF = 3072
ROT = 16
ROW = 2048
DOC_DEV = 2


def shifted(block, axis, distance):
    devices = range(lax.axis_size(axis))
    route = [(i - distance, i) for i in devices if i - distance in devices]
    return lax.ppermute(block, axis, route)


def norm_parts(values, gain, bias):
    middle = jnp.mean(values, -1, keepdims=True)
    centred = values - middle
    factor = lax.rsqrt(jnp.mean(centred * centred, -1, keepdims=True) + 1e-05)
    normed = centred * factor
    return (normed * gain + bias, normed, factor)


def norm_back(grad, gain, normed, factor):
    inner = grad * gain
    return factor * (
        inner
        - jnp.mean(inner, -1, keepdims=True)
        - normed * jnp.mean(inner * normed, -1, keepdims=True)
    )


def rotary_tables(positions):
    half = ROT // 2
    inverse = 10000.0 ** (-(2.0 * jnp.arange(half, dtype=jnp.float32)) / ROT)
    angles = positions.astype(jnp.float32)[:, None] * inverse[None, :]
    cosine = jnp.cos(angles)
    sine = jnp.sin(angles)
    return (jnp.concatenate([cosine, cosine], -1), jnp.concatenate([sine, sine], -1))


def rotate(values, cosine, sine):
    half = ROT // 2
    part = values[..., :ROT]
    turned = jnp.concatenate([-part[..., half:], part[..., :half]], -1)
    moved = part * cosine[:, None, :] + turned * sine[:, None, :]
    return jnp.concatenate([moved, values[..., ROT:]], -1)


def rotate_back(grad, cosine, sine):
    half = ROT // 2
    part = grad[..., :ROT]
    upper = part * sine[:, None, :]
    turned = jnp.concatenate([upper[..., half:], -upper[..., :half]], -1)
    moved = part * cosine[:, None, :] + turned
    return jnp.concatenate([moved, grad[..., ROT:]], -1)


def gelu_slope(pre):
    return 0.5 * (1.0 + lax.erf(pre / math.sqrt(2.0))) + pre * jnp.exp(
        -0.5 * pre * pre
    ) / math.sqrt(2.0 * math.pi)


def per_device(
    tokens,
    seg_ids,
    out_grad,
    first_gain,
    first_bias,
    second_gain,
    second_bias,
    qkv_weight,
    qkv_bias,
    dense_weight,
    up_weight,
    up_bias,
    down_weight,
    out_bias,
):
    rows = tokens.shape[0]
    gathered = (
        lax.all_gather(first_gain, "fsdp", axis=0, tiled=True),
        lax.all_gather(first_bias, "fsdp", axis=0, tiled=True),
        lax.all_gather(second_gain, "fsdp", axis=0, tiled=True),
        lax.all_gather(second_bias, "fsdp", axis=0, tiled=True),
        lax.all_gather(qkv_weight, "fsdp", axis=0, tiled=True),
        lax.all_gather(qkv_bias, "fsdp", axis=0, tiled=True),
        lax.all_gather(dense_weight, "fsdp", axis=0, tiled=True),
        lax.all_gather(up_weight, "fsdp", axis=0, tiled=True),
        lax.all_gather(up_bias, "fsdp", axis=0, tiled=True),
        lax.all_gather(down_weight, "fsdp", axis=0, tiled=True),
        lax.all_gather(out_bias, "fsdp", axis=0, tiled=True),
    )
    (
        gain_first,
        shift_first,
        gain_second,
        shift_second,
        qkv_mat,
        qkv_add,
        dense_mat,
        up_mat,
        up_add,
        down_mat,
        out_add,
    ) = gathered
    stream = tokens.astype(jnp.float32)
    first_full, first_normed, first_factor = norm_parts(
        stream, gain_first.astype(jnp.float32), shift_first.astype(jnp.float32)
    )
    second_full, second_normed, second_factor = norm_parts(
        stream, gain_second.astype(jnp.float32), shift_second.astype(jnp.float32)
    )
    first_in = first_full.astype(jnp.bfloat16)
    second_in = second_full.astype(jnp.bfloat16)
    projected = (
        jnp.dot(first_in, qkv_mat, preferred_element_type=jnp.float32) + qkv_add.astype(jnp.float32)
    ).reshape(rows, H, 3, HD)
    offset = lax.axis_index(("dp", "fsdp")) * rows
    query_pos = offset + jnp.arange(rows, dtype=jnp.int32)
    cosine, sine = rotary_tables(query_pos % ROW)
    scale = 1.0 / math.sqrt(HD)
    query = (rotate(projected[:, :, 0], cosine, sine) * scale).astype(jnp.bfloat16)
    key = rotate(projected[:, :, 1], cosine, sine).astype(jnp.bfloat16)
    value = projected[:, :, 2].astype(jnp.bfloat16)
    key_flat = key.reshape(rows, D)
    value_flat = value.reshape(rows, D)
    earlier = []
    for distance in (2, 1):
        earlier.append(shifted((key_flat, value_flat, seg_ids), ("dp", "fsdp"), distance))
    keys_all = jnp.concatenate([earlier[0][0], earlier[1][0], key_flat], 0)
    values_all = jnp.concatenate([earlier[0][1], earlier[1][1], value_flat], 0)
    docs_all = jnp.concatenate([earlier[0][2], earlier[1][2], seg_ids], 0)
    key_pos = offset - 2 * rows + jnp.arange(3 * rows, dtype=jnp.int32)
    query_heads = query.transpose(1, 0, 2)
    key_heads = keys_all.reshape(3 * rows, H, HD).transpose(1, 0, 2)
    value_heads = values_all.reshape(3 * rows, H, HD).transpose(1, 0, 2)
    width = min(512, rows)
    span = 2 * rows + width
    masks = []
    masks.append(
        (seg_ids[0:width, None] == docs_all[None, 0:span])
        & (key_pos[None, 0:span] <= query_pos[0:width, None])
        & (key_pos[None, 0:span] >= 0)
    )

    def head_forward(operands):
        query_one, key_one, value_one = operands
        scores = jnp.einsum("qd,kd->qk", query_one, key_one, preferred_element_type=jnp.float32)
        scores = jnp.where(masks[0], scores, -1e30)
        top = jnp.max(scores, -1, keepdims=True)
        weights = jnp.where(masks[0], jnp.exp(scores - top), 0.0)
        total = jnp.sum(weights, -1, keepdims=True)
        probs = (weights / total).astype(jnp.bfloat16)
        outputs = [jnp.dot(probs, value_one, preferred_element_type=jnp.float32)]
        totals = [(top + jnp.log(total))[:, 0]]
        return (jnp.concatenate(outputs, 0), jnp.concatenate(totals, 0))

    context_heads, log_totals = lax.map(head_forward, (query_heads, key_heads, value_heads))
    context = context_heads.transpose(1, 0, 2).reshape(rows, D).astype(jnp.bfloat16)
    pre = jnp.dot(second_in, up_mat, preferred_element_type=jnp.float32) + up_add.astype(
        jnp.float32
    )
    activation = jax.nn.gelu(pre, approximate=False).astype(jnp.bfloat16)
    result = (
        stream
        + jnp.dot(context, dense_mat, preferred_element_type=jnp.float32)
        + jnp.dot(activation, down_mat, preferred_element_type=jnp.float32)
        + out_add.astype(jnp.float32)
    )
    output = result.astype(jnp.bfloat16)
    back_weights = (
        lax.all_gather(first_gain, "fsdp", axis=0, tiled=True),
        lax.all_gather(second_gain, "fsdp", axis=0, tiled=True),
        lax.all_gather(qkv_weight, "fsdp", axis=0, tiled=True),
        lax.all_gather(dense_weight, "fsdp", axis=0, tiled=True),
        lax.all_gather(up_weight, "fsdp", axis=0, tiled=True),
        lax.all_gather(down_weight, "fsdp", axis=0, tiled=True),
    )
    back_first, back_second, back_qkv, back_dense, back_up, back_down = back_weights
    cotangent = out_grad.astype(jnp.float32)
    out_bias_grad = jnp.sum(cotangent, 0)
    down_weight_grad = jnp.einsum(
        "tf,td->fd", activation, out_grad, preferred_element_type=jnp.float32
    )
    dense_weight_grad = jnp.einsum(
        "tc,td->cd", context, out_grad, preferred_element_type=jnp.float32
    )
    hidden_grad = jnp.einsum("td,fd->tf", out_grad, back_down, preferred_element_type=jnp.float32)
    pre_grad = (hidden_grad * gelu_slope(pre)).astype(jnp.bfloat16)
    up_weight_grad = jnp.einsum(
        "tc,tf->cf", second_in, pre_grad, preferred_element_type=jnp.float32
    )
    up_bias_grad = jnp.sum(pre_grad.astype(jnp.float32), 0)
    second_grad = jnp.einsum("tf,cf->tc", pre_grad, back_up, preferred_element_type=jnp.float32)
    context_grad = jnp.einsum(
        "td,cd->tc", out_grad, back_dense, preferred_element_type=jnp.float32
    ).astype(jnp.bfloat16)
    context_grad_heads = context_grad.reshape(rows, H, HD).transpose(1, 0, 2)

    def head_backward(operands):
        query_one, key_one, value_one, grad_one, total_one = operands
        key_acc = jnp.zeros((3 * rows, HD), jnp.float32)
        value_acc = jnp.zeros((3 * rows, HD), jnp.float32)
        scores = jnp.einsum("qd,kd->qk", query_one, key_one, preferred_element_type=jnp.float32)
        weights = jnp.where(masks[0], jnp.exp(scores - total_one[0:width, None]), 0.0)
        probs_grad = jnp.einsum(
            "qd,kd->qk", grad_one, value_one, preferred_element_type=jnp.float32
        )
        score_grad = (
            weights * (probs_grad - jnp.sum(weights * probs_grad, -1, keepdims=True))
        ).astype(jnp.bfloat16)
        query_parts = [jnp.dot(score_grad, key_one, preferred_element_type=jnp.float32)]
        key_acc = key_acc.at[0:span].add(
            jnp.einsum("qk,qd->kd", score_grad, query_one, preferred_element_type=jnp.float32)
        )
        value_acc = value_acc.at[0:span].add(
            jnp.einsum(
                "qk,qd->kd",
                weights.astype(jnp.bfloat16),
                grad_one,
                preferred_element_type=jnp.float32,
            )
        )
        return (jnp.concatenate(query_parts, 0), key_acc, value_acc)

    query_grad_heads, key_grad_heads, value_grad_heads = lax.map(
        head_backward, (query_heads, key_heads, value_heads, context_grad_heads, log_totals)
    )
    key_grad_all = key_grad_heads.transpose(1, 0, 2).reshape(3 * rows, D)
    value_grad_all = value_grad_heads.transpose(1, 0, 2).reshape(3 * rows, D)
    key_grad_own = key_grad_all[2 * rows :]
    value_grad_own = value_grad_all[2 * rows :]
    for distance in (2, 1):
        lower = (2 - distance) * rows
        returned = shifted(
            (key_grad_all[lower : lower + rows], value_grad_all[lower : lower + rows]),
            ("dp", "fsdp"),
            -distance,
        )
        key_grad_own = key_grad_own + returned[0]
        value_grad_own = value_grad_own + returned[1]
    query_grad = rotate_back(query_grad_heads.transpose(1, 0, 2) * scale, cosine, sine)
    key_grad = rotate_back(key_grad_own.reshape(rows, H, HD), cosine, sine)
    projected_grad = (
        jnp.stack([query_grad, key_grad, value_grad_own.reshape(rows, H, HD)], 2)
        .reshape(rows, 3 * D)
        .astype(jnp.bfloat16)
    )
    qkv_weight_grad = jnp.einsum(
        "tc,tk->ck", first_in, projected_grad, preferred_element_type=jnp.float32
    )
    qkv_bias_grad = jnp.sum(projected_grad.astype(jnp.float32), 0)
    first_grad = jnp.einsum(
        "tk,ck->tc", projected_grad, back_qkv, preferred_element_type=jnp.float32
    )
    input_full = (
        cotangent
        + norm_back(first_grad, back_first.astype(jnp.float32), first_normed, first_factor)
        + norm_back(second_grad, back_second.astype(jnp.float32), second_normed, second_factor)
    )
    input_grad = input_full.astype(jnp.bfloat16)
    first_gain_grad = jnp.sum(first_grad * first_normed, 0)
    first_bias_grad = jnp.sum(first_grad, 0)
    second_gain_grad = jnp.sum(second_grad * second_normed, 0)
    second_bias_grad = jnp.sum(second_grad, 0)
    shares = (
        lax.psum_scatter(first_gain_grad, "fsdp", scatter_dimension=0, tiled=True),
        lax.psum_scatter(first_bias_grad, "fsdp", scatter_dimension=0, tiled=True),
        lax.psum_scatter(second_gain_grad, "fsdp", scatter_dimension=0, tiled=True),
        lax.psum_scatter(second_bias_grad, "fsdp", scatter_dimension=0, tiled=True),
        lax.psum_scatter(qkv_weight_grad, "fsdp", scatter_dimension=0, tiled=True),
        lax.psum_scatter(qkv_bias_grad, "fsdp", scatter_dimension=0, tiled=True),
        lax.psum_scatter(dense_weight_grad, "fsdp", scatter_dimension=0, tiled=True),
        lax.psum_scatter(up_weight_grad, "fsdp", scatter_dimension=0, tiled=True),
        lax.psum_scatter(up_bias_grad, "fsdp", scatter_dimension=0, tiled=True),
        lax.psum_scatter(down_weight_grad, "fsdp", scatter_dimension=0, tiled=True),
        lax.psum_scatter(out_bias_grad, "fsdp", scatter_dimension=0, tiled=True),
    )
    (
        share_fg,
        share_fb,
        share_sg,
        share_sb,
        share_qw,
        share_qb,
        share_dw,
        share_uw,
        share_ub,
        share_ow,
        share_ob,
    ) = shares
    summed = lax.psum(
        (
            share_fg,
            share_fb,
            share_sg,
            share_sb,
            share_qw,
            share_qb,
            share_dw,
            share_uw,
            share_ub,
            share_ow,
            share_ob,
        ),
        "dp",
    )
    doc_total = DOC_DEV * lax.axis_size("dp") * lax.axis_size("fsdp")
    token_norm = (
        jnp.sum(jnp.square(activation.astype(jnp.float32)), -1)
        * jnp.sum(cotangent * cotangent, -1)
        / (FF * D)
    )
    member = (seg_ids[:, None] == jnp.arange(doc_total, dtype=jnp.int32)[None, :]).astype(
        jnp.float32
    )
    doc_sums = jnp.dot(token_norm, member, precision=lax.Precision.HIGHEST)
    doc_counts = jnp.sum(member, 0)
    totals = lax.psum((doc_sums, doc_counts), ("dp", "fsdp"))
    doc_norms = totals[0] / totals[1]
    return (
        output,
        input_grad,
        summed[0],
        summed[1],
        summed[2],
        summed[3],
        summed[4],
        summed[5],
        summed[6],
        summed[7],
        summed[8],
        summed[9],
        summed[10],
        doc_norms,
    )


def solution(mesh):
    in_specs = (
        P(("dp", "fsdp"), None),
        P(("dp", "fsdp")),
        P(("dp", "fsdp"), None),
        P("fsdp"),
        P("fsdp"),
        P("fsdp"),
        P("fsdp"),
        P("fsdp", None),
        P("fsdp"),
        P("fsdp", None),
        P("fsdp", None),
        P("fsdp"),
        P("fsdp", None),
        P("fsdp"),
    )
    out_specs = (
        P(("dp", "fsdp"), None),
        P(("dp", "fsdp"), None),
        P("fsdp"),
        P("fsdp"),
        P("fsdp"),
        P("fsdp"),
        P("fsdp", None),
        P("fsdp"),
        P("fsdp", None),
        P("fsdp", None),
        P("fsdp"),
        P("fsdp", None),
        P("fsdp"),
        P(),
    )
    return jax.shard_map(
        per_device, mesh=mesh, in_specs=in_specs, out_specs=out_specs, check_vma=False
    )
```

profile of v0, /device:TPU:1, one launch (start us, length us, event | category | flops | bytes accessed | tf_op | source)
XLA Modules:
  0.0 1191.7 jit_solution(334832693091773935)
XLA Ops:
  9.5 4.0 collective-permute-start.2
  13.6 3.1 collective-permute-start.3
  22.7 31.7 %all-reduce.17 = (bf16[768]{0:T(1024)(128)(2,1)S(1)}, bf16[768]{0:T(1024)(128)(2,1)S(1)}, bf16[2304]{0:T(1024)(128)(2,1)S(1)}, bf16[768]{0:T(1024)(128)(2,1)S(1)...) all-reduce(bf16[768]{0:T(1024)(128)(2,1)S(1)} %dynamic-update-slice, ...), channel_id=1, replica_groups=mesh['dp'=4,'fsdp'=8] {'fsdp'}, use_global_device_ids=true, to_apply=%add.4 | all-reduce | flops 6144 | bytes 24576
  57.7 61.3 %all-gather.6.cloned.1.call-done = bf16[768,2304]{1,0:T(8,128)(2,1)} async-done(((bf16[96,2304]{1,0:T(8,128)(2,1)}), bf16[768,2304]{1,0:T(8,128)(2,1)}) %all-gather.6.cloned.1.call-update) | async-done | bytes 3538960 | tf_op jit(solution)/shard_map/all_gather | solution.py:94
  119.0 6.3 convolution_add_fusion
  125.3 6.1 copy.70
  141.2 3.3 collective-permute-start
  144.5 4.0 collective-permute-start.1
  152.0 16.9 %collective-permute-done.4 = bf16[512,768]{0,1:T(8,128)(2,1)S(1)} collective-permute-done((bf16[512,768]{0,1:T(8,128)(2,1)}, bf16[512,768]{0,1:T(8,128)(2,1)S(1)}, u32[]{:S(2)}, u32[]{:S(2)}) %collective-permute-start.4) | collective-permute-done | bytes 786464 | tf_op jit(solution)/shard_map/ppermute | solution.py:20
  168.9 31.4 %collective-permute-done.5 = bf16[512,768]{0,1:T(8,128)(2,1)} collective-permute-done((bf16[512,768]{0,1:T(8,128)(2,1)}, bf16[512,768]{0,1:T(8,128)(2,1)}, u32[]{:S(2)}, u32[]{:S(2)}) %collective-permute-start.5) | collective-permute-done | bytes 786464 | tf_op jit(solution)/shard_map/ppermute | solution.py:20
  201.9 3.9 copy.74
  205.8 52.5 %collective-permute-done.1 = bf16[512,768]{0,1:T(8,128)(2,1)} collective-permute-done((bf16[512,768]{0,1:T(8,128)(2,1)S(1)}, bf16[512,768]{0,1:T(8,128)(2,1)}, u32[]{:S(2)}, u32[]{:S(2)}) %collective-permute-start.1) | collective-permute-done | bytes 786464 | tf_op jit(solution)/shard_map/ppermute | solution.py:20
  259.9 4.0 copy.73
  263.9 82.0 %while.37 = (s32[]{:T(128)}, bf16[12,512,64]{1,2,0:T(8,128)(2,1)}, f32[12,512]{1,0:T(8,128)S(1)}, bf16[12,512,64]{2,1,0:T(8,128)(2,1)}, bf16[12,1536,64]{2,1,0:T...) while((s32[]{:T(128)}, bf16[12,512,64]{1,2,0:T(8,128)(2,1)}, ...), condition=%wide.region_5.6_spmd.clone.clone, body=%wide.region_2.5_spmd.clone.sunk.clone | while | flops 217841152 | bytes 10562161 | solution.py:167
  267.7 3.1 fusion.173
  274.5 3.1 fusion.173
  281.3 3.1 fusion.173
  288.2 3.1 fusion.173
  301.9 3.1 fusion.173
  315.5 3.1 fusion.173
  322.4 3.1 fusion.173
  329.2 3.1 fusion.173
  336.0 3.1 fusion.173
  342.8 3.1 fusion.173
  345.9 3.7 fusion.113
  349.7 124.3 %while.38 = (s32[]{:T(128)}, f32[12,512,64]{1,2,0:T(8,128)S(1)}, f32[12,1536,64]{1,2,0:T(8,128)}, f32[12,1536,64]{1,2,0:T(8,128)}, bf16[12,512,64]{2,1,0:T(8,128...) while((s32[]{:T(128)}, f32[12,512,64]{1,2,0:T(8,128)S(1)}, ...), condition=%wide.region_8.9_spmd.clone.clone, body=%wide.region_6.8_spmd.clone.sunk.clone | while | flops 512753152 | bytes 26116744 | solution.py:235
  474.1 3.4 fusion.106
  477.4 3.3 collective-permute-start.6
  486.2 4.4 collective-permute-start.9
  490.6 25.2 %collective-permute-done.6 = f32[512,768]{0,1:T(8,128)S(1)} collective-permute-done((f32[512,768]{0,1:T(8,128)S(1)}, f32[512,768]{0,1:T(8,128)S(1)}, u32[]{:S(2)}, u32[]{:S(2)}) %collective-permute-start.6) | collective-permute-done | bytes 1572896 | tf_op jit(solution)/shard_map/ppermute | solution.py:20
  515.8 3.3 collective-permute-done.7
  520.2 62.7 %collective-permute-done.8 = f32[512,768]{0,1:T(8,128)S(1)} collective-permute-done((f32[512,768]{0,1:T(8,128)S(1)}, f32[512,768]{0,1:T(8,128)S(1)}, u32[]{:S(2)}, u32[]{:S(2)}) %collective-permute-start.8) | collective-permute-done | bytes 1572896 | tf_op jit(solution)/shard_map/ppermute | solution.py:20
  585.6 5.3 fusion.101
  591.5 57.8 %all-gather = bf16[8,1,384]{2,1,0:T(2,128)(2,1)S(1)} all-gather(bf16[1,1,384]{2,1,0:T(2,128)(2,1)S(1)} %reshape.249), channel_id=1, replica_groups=mesh['dp'=4,'fsdp'=8] {'fsdp'}, dimensions={0}, use_global_device_ids=true | all-gather | bytes 6912 | tf_op jit(solution)/shard_map/all_gather | solution.py:98
  649.3 20.2 %multiply_reduce_fusion.1 = (f32[512]{0:T(512)S(1)}, bf16[512,3072]{1,0:T(8,128)(2,1)}, f32[512,3072]{1,0:T(8,128)}) fusion(f32[3072]{0:T(1024)S(1)} %bitcast.214, bf16[768,3072]{1,0:T(8,128)(2,1)} %all-gather.10.cloned.1.call-done, bf16[512,768]{1,0:T(8,128)(2,1)S(1)} %copy-done.1, f32[768]{0:T(1024)S(1)} %convert_element_type.141, ...), kind=kOutput, calls=%fused_computation.64 | convolution fusion | flops 2526805504 | bytes 14966784 | tf_op jit(solution)/shard_map/dot_general | solution.py:169
  669.6 7.1 convert_reduce_fusion
  678.4 5.5 fusion.97
  683.9 8.2 fusion.114
  694.5 6.0 fusion.111
  702.7 5.1 fusion.112
  707.9 46.3 %reduce-scatter.5.cloned.1.call-done = f32[96,2304]{1,0:T(8,128)} async-done(((f32[768,2304]{1,0:T(8,128)}), f32[96,2304]{1,0:T(8,128)}) %reduce-scatter.5.cloned.1.call-update) | async-done | bytes 884752 | tf_op jit(solution)/shard_map/reduce_scatter | solution.py:280
  754.2 167.3 %reduce-scatter.9.cloned.1.call-done = f32[96,3072]{1,0:T(8,128)} async-done(((f32[768,3072]{1,0:T(8,128)}), f32[96,3072]{1,0:T(8,128)}) %reduce-scatter.9.cloned.1.call-update) | async-done | bytes 1179664 | tf_op jit(solution)/shard_map/reduce_scatter | solution.py:283
  921.5 166.6 %reduce-scatter.11.cloned.1.call-done = f32[384,768]{1,0:T(8,128)} async-done(((f32[3072,768]{1,0:T(8,128)}), f32[384,768]{1,0:T(8,128)}) %reduce-scatter.11.cloned.1.call-update) | async-done | bytes 1179664 | tf_op jit(solution)/shard_map/reduce_scatter | solution.py:285
  1088.2 6.6 fusion.81
  1094.9 3.5 fusion.87
  1098.4 28.5 %all-reduce.14 = (f32[768]{0:T(1024)S(1)}, f32[768]{0:T(1024)S(1)}, f32[768]{0:T(1024)S(1)}, f32[768]{0:T(1024)S(1)}, f32[2304]{0:T(1024)S(1)}, /*index=5*/f32[3072]{0:T(1024)S(1)}, f32[768]{0:T(1024)S(1)}) all-reduce(f32[768]{0:T(1024)S(1)} %get-tuple-element.449, ...), channel_id=2, replica_groups=mesh['dp'=4,'fsdp'=8] {'fsdp'}, use_global_device_ids=true, to_apply=%region_14.15.clone | all-reduce | flops 9216 | bytes 73728
  1127.4 43.2 %all-reduce.13 = (f32[64]{0:T(128)S(1)}, f32[64]{0:T(128)S(1)}) all-reduce(f32[64]{0:T(128)S(1)} %convolution_bitcast_fusion.3, f32[64]{0:T(128)S(1)} %convert_reduce_fusion.4), channel_id=1, replica_groups=mesh['dp'=4,'fsdp'=8] {'dp','fsdp'}, use_global_device_ids=true, to_apply=%region_44.45 | all-reduce | flops 128 | bytes 1024 | tf_op jit(solution)/shard_map/psum | solution.py:328
  1171.2 7.8 all-reduce.15
  (306 shorter events, 222.6 us)
Async XLA Ops:
  7.2 47.3 %copy-start.12 = (s32[512]{0:T(512)S(1)}, s32[512]{0:T(512)}, u32[]{:S(2)}) copy-start(s32[512]{0:T(512)} %param.27) | copy-start | bytes 6148
  7.2 13.3 %copy-start = (bf16[512,768]{1,0:T(8,128)(2,1)S(1)}, bf16[512,768]{1,0:T(8,128)(2,1)}, u32[]{:S(2)}) copy-start(bf16[512,768]{1,0:T(8,128)(2,1)} %param.26) | copy-start | bytes 2359300
  7.2 14.0 %copy-start.17 = (bf16[96]{0:T(256)(128)(2,1)S(1)}, bf16[96]{0:T(256)(128)(2,1)}, u32[]{:S(2)}) copy-start(bf16[96]{0:T(256)(128)(2,1)} %param.29) | copy-start | bytes 580
  7.2 14.3 %copy-start.18 = (bf16[96]{0:T(256)(128)(2,1)S(1)}, bf16[96]{0:T(256)(128)(2,1)}, u32[]{:S(2)}) copy-start(bf16[96]{0:T(256)(128)(2,1)} %param.30) | copy-start | bytes 580
  7.2 14.5 %copy-start.19 = (bf16[96]{0:T(256)(128)(2,1)S(1)}, bf16[96]{0:T(256)(128)(2,1)}, u32[]{:S(2)}) copy-start(bf16[96]{0:T(256)(128)(2,1)} %param.31) | copy-start | bytes 580
  7.2 14.7 %copy-start.20 = (bf16[96]{0:T(256)(128)(2,1)S(1)}, bf16[96]{0:T(256)(128)(2,1)}, u32[]{:S(2)}) copy-start(bf16[96]{0:T(256)(128)(2,1)} %param.32) | copy-start | bytes 580
  7.2 14.9 %copy-start.21 = (bf16[96]{0:T(256)(128)(2,1)S(1)}, bf16[96]{0:T(256)(128)(2,1)}, u32[]{:S(2)}) copy-start(bf16[96]{0:T(256)(128)(2,1)} %param.39) | copy-start | bytes 580
  7.3 15.2 %copy-start.14 = (bf16[288]{0:T(512)(128)(2,1)S(1)}, bf16[288]{0:T(512)(128)(2,1)}, u32[]{:S(2)}) copy-start(bf16[288]{0:T(512)(128)(2,1)} %param.34) | copy-start | bytes 1732
  7.3 47.2 %copy-start.4 = (bf16[512,768]{1,0:T(8,128)(2,1)S(1)}, bf16[512,768]{1,0:T(8,128)(2,1)}, u32[]{:S(2)}) copy-start(bf16[512,768]{1,0:T(8,128)(2,1)} %param.28) | copy-start | bytes 2359300
  7.3 47.2 %all-gather.8.cloned.1.call-start = ((), (), s32[]{:S(2)}) async-start(), calls=%async_computation.5 | async-start | bytes 1327104 | tf_op jit(solution)/shard_map/all_gather | solution.py:96
  8.0 111.0 %all-gather.6.cloned.1.call-start = ((), (), s32[]{:S(2)}) async-start(), calls=%async_computation.4 | async-start | bytes 3981312 | tf_op jit(solution)/shard_map/all_gather | solution.py:94
  8.8 640.6 %all-gather.10.cloned.1.call-start = ((), (), s32[]{:S(2)}) async-start(), calls=%async_computation.6 | async-start | bytes 5308416 | tf_op jit(solution)/shard_map/all_gather | solution.py:97
  9.5 660.1 %all-gather.12.cloned.1.call-start = ((), (), s32[]{:S(2)}) async-start(), calls=%async_computation.7 | async-start | bytes 5308416 | tf_op jit(solution)/shard_map/all_gather | solution.py:99
  9.5 44.9 %collective-permute-start.2 = (s32[512]{0:T(512)}, s32[512]{0:T(512)S(1)}, u32[]{:S(2)}, u32[]{:S(2)}) collective-permute-start(s32[512]{0:T(512)} %param.27), channel_id=1, source_target_pairs={{0,2},{1,3},{2,4},{3,5},{4,6},{5,7},{6,8},{7,9},{8,10},{9,11},{10,... | collective-permute-start | bytes 6152 | tf_op jit(solution)/shard_map/ppermute | solution.py:20
  13.6 40.8 %collective-permute-start.3 = (s32[512]{0:T(512)}, s32[512]{0:T(512)S(1)}, u32[]{:S(2)}, u32[]{:S(2)}) collective-permute-start(s32[512]{0:T(512)} %param.27), channel_id=1, source_target_pairs={{0,1},{1,2},{2,3},{3,4},{4,5},{5,6},{6,7},{7,8},{8,9},{9,10},{10,1... | collective-permute-start | bytes 6152 | tf_op jit(solution)/shard_map/ppermute | solution.py:20
  16.8 691.1 %reduce-scatter.7.cloned.1.call-start = ((), (), s32[]{:S(2)}) async-start(), calls=%async_computation.9 | async-start | bytes 2654208 | tf_op jit(solution)/shard_map/reduce_scatter | solution.py:282
  133.8 35.0 %collective-permute-start.4 = (bf16[512,768]{0,1:T(8,128)(2,1)}, bf16[512,768]{0,1:T(8,128)(2,1)S(1)}, u32[]{:S(2)}, u32[]{:S(2)}) collective-permute-start(bf16[512,768]{0,1:T(8,128)(2,1)} %bitcast.10), channel_id=1, source_target_pairs={{0,2},{1,3},{2,4},{3,5},{4,6},{5,7},{6,8},{7,9},{8,10},{9,11},{10,... | collective-permute-start | bytes 2359304 | tf_op jit(solution)/shard_map/ppermute | solution.py:20
  136.3 63.9 %collective-permute-start.5 = (bf16[512,768]{0,1:T(8,128)(2,1)}, bf16[512,768]{0,1:T(8,128)(2,1)}, u32[]{:S(2)}, u32[]{:S(2)}) collective-permute-start(bf16[512,768]{0,1:T(8,128)(2,1)} %bitcast.10), channel_id=1, source_target_pairs={{0,1},{1,2},{2,3},{3,4},{4,5},{5,6},{6,7},{7,8},{8,9},{9,10},{10,1... | collective-permute-start | bytes 2359304 | tf_op jit(solution)/shard_map/ppermute | solution.py:20
  141.2 64.6 %collective-permute-start = (bf16[512,768]{0,1:T(8,128)(2,1)S(1)}, bf16[512,768]{0,1:T(8,128)(2,1)}, u32[]{:S(2)}, u32[]{:S(2)}) collective-permute-start(bf16[512,768]{0,1:T(8,128)(2,1)S(1)} %bitcast.199), channel_id=1, source_target_pairs={{0,2},{1,3},{2,4},{3,5},{4,6},{5,7},{6,8},{7,9},{8,10},{9,11},{10,... | collective-permute-start | bytes 2359304 | tf_op jit(solution)/shard_map/ppermute | solution.py:20
  144.5 113.8 %collective-permute-start.1 = (bf16[512,768]{0,1:T(8,128)(2,1)S(1)}, bf16[512,768]{0,1:T(8,128)(2,1)}, u32[]{:S(2)}, u32[]{:S(2)}) collective-permute-start(bf16[512,768]{0,1:T(8,128)(2,1)S(1)} %bitcast.200), channel_id=1, source_target_pairs={{0,1},{1,2},{2,3},{3,4},{4,5},{5,6},{6,7},{7,8},{8,9},{9,10},{10,1... | collective-permute-start | bytes 2359304 | tf_op jit(solution)/shard_map/ppermute | solution.py:20
  168.9 31.4 %copy-start.11 = (bf16[512,768]{0,1:T(8,128)(2,1)}, bf16[512,768]{0,1:T(8,128)(2,1)S(1)}, u32[]{:S(2)}) copy-start(bf16[512,768]{0,1:T(8,128)(2,1)S(1)} %collective-permute-done.4) | copy-start | bytes 2359300
  345.9 3.8 copy-start.8
  349.7 404.5 %reduce-scatter.5.cloned.1.call-start = ((), (), s32[]{:S(2)}) async-start(), calls=%async_computation.8 | async-start | bytes 7962624 | tf_op jit(solution)/shard_map/reduce_scatter | solution.py:280
  474.0 9.0 slice-start
  474.0 9.0 slice-start.1
  477.4 38.4 %collective-permute-start.6 = (f32[512,768]{0,1:T(8,128)S(1)}, f32[512,768]{0,1:T(8,128)S(1)}, u32[]{:S(2)}, u32[]{:S(2)}) collective-permute-start(f32[512,768]{0,1:T(8,128)S(1)} %bitcast.210), channel_id=1, source_target_pairs={{2,0},{3,1},{4,2},{5,3},{6,4},{7,5},{8,6},{9,7},{10,8},{11,9},{12,... | collective-permute-start | bytes 4718600 | tf_op jit(solution)/shard_map/ppermute | solution.py:20
  480.7 38.4 %collective-permute-start.7 = (f32[512,768]{0,1:T(8,128)S(1)}, f32[512,768]{0,1:T(8,128)S(1)}, u32[]{:S(2)}, u32[]{:S(2)}) collective-permute-start(f32[512,768]{0,1:T(8,128)S(1)} %bitcast.209), channel_id=1, source_target_pairs={{1,0},{2,1},{3,2},{4,3},{5,4},{6,5},{7,6},{8,7},{9,8},{10,9},{11,1... | collective-permute-start | bytes 4718600 | tf_op jit(solution)/shard_map/ppermute | solution.py:20
  483.8 99.1 %collective-permute-start.8 = (f32[512,768]{0,1:T(8,128)S(1)}, f32[512,768]{0,1:T(8,128)S(1)}, u32[]{:S(2)}, u32[]{:S(2)}) collective-permute-start(f32[512,768]{0,1:T(8,128)S(1)} %bitcast.208), channel_id=1, source_target_pairs={{2,0},{3,1},{4,2},{5,3},{6,4},{7,5},{8,6},{9,7},{10,8},{11,9},{12,... | collective-permute-start | bytes 4718600 | tf_op jit(solution)/shard_map/ppermute | solution.py:20
  486.2 96.7 %collective-permute-start.9 = (f32[512,768]{0,1:T(8,128)S(1)}, f32[512,768]{0,1:T(8,128)S(1)}, u32[]{:S(2)}, u32[]{:S(2)}) collective-permute-start(f32[512,768]{0,1:T(8,128)S(1)} %bitcast.207), channel_id=1, source_target_pairs={{1,0},{2,1},{3,2},{4,3},{5,4},{6,5},{7,6},{8,7},{9,8},{10,9},{11,1... | collective-permute-start | bytes 4718600 | tf_op jit(solution)/shard_map/ppermute | solution.py:20
  583.9 1.7 copy-start.1
  584.2 1.4 copy-start.7
  590.8 0.7 copy-start.15
  590.9 330.7 %reduce-scatter.9.cloned.1.call-start = ((), (), s32[]{:S(2)}) async-start(), calls=%async_computation.10 | async-start | bytes 10616832 | tf_op jit(solution)/shard_map/reduce_scatter | solution.py:283
  649.3 20.3 %copy-start.5 = (bf16[512,768]{1,0:T(8,128)(2,1)S(1)}, bf16[512,768]{1,0:T(8,128)(2,1)}, u32[]{:S(2)}) copy-start(bf16[512,768]{1,0:T(8,128)(2,1)} %param.28) | copy-start | bytes 2359300
  676.7 1.6 copy-start.2
  683.9 404.3 %reduce-scatter.11.cloned.1.call-start = ((), (), s32[]{:S(2)}) async-start(), calls=%async_computation.11 | async-start | bytes 10616832 | tf_op jit(solution)/shard_map/reduce_scatter | solution.py:285
  692.1 2.2 copy-start.13
  692.2 486.8 %all-reduce.20.cloned.1.call-start = ((), (), s32[]{:S(2)}) async-start(), calls=%async_computation.12 | async-start | bytes 7077888 | tf_op jit(solution)/shard_map/psum | solution.py:301
  694.5 6.0 copy-start.6
  694.5 6.1 copy-start.16
  700.5 2.2 copy-start.3
  1179.0 4.0 copy-start.10
  1179.0 5.0 copy-start.9
Sparse Core Ops, SparseCore 0:
  10.3 42.2 all-gather.7
  54.8 64.2 all-gather.5
  121.2 104.3 all-gather.9
  227.6 99.0 all-gather.11
  349.8 65.9 reduce-scatter.6
  591.0 163.1 reduce-scatter.4
  758.2 163.2 reduce-scatter.8
  925.6 162.5 reduce-scatter.10
  1090.9 75.0 all-reduce.19
where the time goes:
time: 1200 us; the launch traced here: 1190 us
  waiting for transfers between devices  636 us (53%)
  matrix products  260 us (22%)
  blocking collectives  169 us (14%)
  local copies, waits for them, and re-layouts  42 us (4%)
  other arithmetic  34.2 us (3%)
  starting transfers between devices  31.8 us (3%)
  between operations  18 us (2%)
    ppermute x10, waiting for transfers between devices, shifted(): return lax.ppermute(block, axis, route)  192 us
    reduce_scatter x1, waiting for transfers between devices, per_device(): lax.psum_scatter(up_weight_grad, 'fsdp', scatter_dimension=0, tiled=True)  167 us
    reduce_scatter x1, waiting for transfers between devices, per_device(): lax.psum_scatter(down_weight_grad, 'fsdp', scatter_dimension=0, tiled=True)  167 us
    all_gather x1, waiting for transfers between devices, per_device(): lax.all_gather(qkv_weight, 'fsdp', axis=0, tiled=True)  61.3 us
    unnamed x2, blocking collectives  60.2 us
    all_gather x1, blocking collectives, per_device(): lax.all_gather(up_bias, 'fsdp', axis=0, tiled=True)  57.8 us
    reduce_scatter x1, waiting for transfers between devices, per_device(): lax.psum_scatter(qkv_weight_grad, 'fsdp', scatter_dimension=0, tiled=True)  46.3 us
    psum x1, blocking collectives, per_device(): totals = lax.psum((doc_sums, doc_counts), ('dp', 'fsdp'))  43.2 us
  transfers between devices with their start and end apart: 19, of which 10 were waited for; matrix products, arithmetic and copies ran while one was open for 27% of the time, Pallas kernels for 0%

commit v1 on v0

v1 whole, which is shorter than its diff:
```python
import functools
import math

import jax
import jax.numpy as jnp
from jax import lax
from jax.experimental import pallas as pl
from jax.experimental.pallas import tpu as pltpu
from jax.sharding import PartitionSpec as P

D = 768
H = 12
HD = 64
FF = 3072
ROT = 16
ROW = 2048
DOC_DEV = 2
LANES = 128
PAIRS = D // LANES
MESH = pl.DeviceIdType.MESH
VMEM_LIMIT = 60 * 1024 * 1024


class Layout:
    def __init__(self, dp, fsdp):
        self.dp, self.fsdp = dp, fsdp
        self.nc = 2
        self.nx = dp // 2
        ny = 1
        while (2 * ny) * (2 * ny) <= fsdp:
            ny *= 2
        self.ny, self.nz = ny, fsdp // ny
        self.sub = max(1, self.nx // 2)
        self.unit = 4 // self.nx
        self.down_unit = 2 // self.sub

    def coords(self):
        d, f = lax.axis_index("dp"), lax.axis_index("fsdp")
        return d // 2, d % 2, f // self.ny, f % self.ny

    def device(self, x, c, z, y):
        return {"dp": x * 2 + c, "fsdp": z * self.ny + y}


def wrap(value, size):
    return lax.rem(value + size, size)


GROUPS = ("att", "up", "down")
CHUNKS = tuple((g, i) for g in range(3) for i in range(3))


def block_shape(lay, group, shard_rows):
    if group < 2:
        return (2, lay.nx, 3, lay.unit, lay.nz, lay.ny, shard_rows, LANES)
    return (3, lay.sub, lay.down_unit, lay.nz, lay.ny, 2, lay.nx // lay.sub, shard_rows, LANES)


def view(lay, ref, group, i, c, x, z, y):
    if group < 2:
        return ref.at[c, x, i, :, z, y]
    if isinstance(x, slice):
        return ref.at[i, :, :, z, y, c, :]
    return ref.at[i, lax.rem(x, lay.sub), :, z, y, c, x // lay.sub]


ALL = slice(None)


def part_shape(lay, group, x_all, z_all, y_all, shard_rows):
    tail = ()
    if z_all:
        tail += (lay.nz,)
    if y_all:
        tail += (lay.ny,)
    if group < 2:
        head = ((lay.nx,) if x_all else ()) + (lay.unit,)
        return head + tail + (shard_rows, LANES)
    if x_all:
        return (lay.sub, lay.down_unit) + tail + (lay.nx // lay.sub, shard_rows, LANES)
    return (lay.down_unit,) + tail + (shard_rows, LANES)


def barrier_with(peers):
    sem = pltpu.get_barrier_semaphore()
    for peer in peers:
        pl.semaphore_signal(sem, inc=1, device_id=peer, device_id_type=MESH)
    pl.semaphore_wait(sem, len(peers))


def line_peers(lay):
    x, c, z, y = lay.coords()
    xs = [lay.device(wrap(x + k, lay.nx), c, z, y) for k in range(1, lay.nx)]
    ys = [lay.device(x, c, z, wrap(y + k, lay.ny)) for k in range(1, lay.ny)]
    zs = [lay.device(x, c, wrap(z + k, lay.nz), y) for k in range(1, lay.nz)]
    cs = [lay.device(x, 1 - c, z, y)]
    return xs, cs, zs, ys


def remote(src, dst, ssem, rsem, device):
    copy = pltpu.make_async_remote_copy(
        src_ref=src, dst_ref=dst, send_sem=ssem, recv_sem=rsem, device_id=device, device_id_type=MESH
    )
    copy.start()
    return copy


def gather_kernel(
    lay, u_att, u_up, u_down, small, tok, seg,
    g_att, g_up, g_down, g_small, tok_halo, seg_halo,
    local_sem, z_s, z_r, y_s, y_r, x_s, x_r, c_s, c_r, sm_s, sm_r, h_s, h_r,
):
    x, c, z, y = lay.coords()
    xs, cs, zs, ys = line_peers(lay)
    total = lay.dp * lay.fsdp
    b = lax.axis_index("dp") * lay.fsdp + lax.axis_index("fsdp")

    def stream(k):
        t = wrap(b + k, total)
        return {"dp": t // lay.fsdp, "fsdp": lax.rem(t, lay.fsdp)}

    around = [stream(2), stream(-2), stream(1), stream(-1)]
    barrier_with(xs + cs + zs + ys + around)
    gs = (g_att, g_up, g_down)
    us = (u_att, u_up, u_down)

    locals_ = [
        pltpu.make_async_copy(u_att.at[c, x], g_att.at[c, x, :, :, z, y], local_sem.at[0]),
        pltpu.make_async_copy(u_up.at[c, x], g_up.at[c, x, :, :, z, y], local_sem.at[1]),
        pltpu.make_async_copy(
            u_down.at[:, lax.rem(x, lay.sub), :, c, x // lay.sub],
            g_down.at[:, lax.rem(x, lay.sub), :, z, y, c, x // lay.sub],
            local_sem.at[2],
        ),
        pltpu.make_async_copy(small, g_small.at[z, y], local_sem.at[3]),
    ]
    for copy in locals_:
        copy.start()
    sends = []
    halo_z = [
        remote(tok, tok_halo.at[0], h_s.at[0], h_r.at[0], around[0]),
        remote(seg, seg_halo.at[0], h_s.at[1], h_r.at[1], around[0]),
        remote(seg, seg_halo.at[1], h_s.at[2], h_r.at[2], around[2]),
    ]
    for copy in locals_:
        copy.wait()
    sends += halo_z
    stage_z, stage_1, stage_2, stage_c = {}, {}, {}, {}
    n = len(CHUNKS)

    def issue_z(t):
        g, i = CHUNKS[t]
        piece = view(lay, gs[g], g, i, c, x, z, y)
        stage_z[t] = [
            remote(piece, piece, z_s.at[t, k], z_r.at[t, k], zs[k]) for k in range(lay.nz - 1)
        ]

    def issue_1(t):
        g, i = CHUNKS[t]
        piece = view(lay, gs[g], g, i, c, x, ALL, y)
        peers, ss, rs = (ys, y_s, y_r) if i < 2 else (xs, x_s, x_r)
        stage_1[t] = [remote(piece, piece, ss.at[t, k], rs.at[t, k], p) for k, p in enumerate(peers)]

    def issue_2(t):
        g, i = CHUNKS[t]
        if i < 2:
            piece = view(lay, gs[g], g, i, c, x, ALL, ALL)
            peers, ss, rs = xs, x_s, x_r
        else:
            piece = view(lay, gs[g], g, i, c, ALL, ALL, y)
            peers, ss, rs = ys, y_s, y_r
        stage_2[t] = [remote(piece, piece, ss.at[t, k], rs.at[t, k], p) for k, p in enumerate(peers)]

    def issue_c(t):
        g, i = CHUNKS[t]
        piece = view(lay, gs[g], g, i, c, ALL, ALL, ALL)
        stage_c[t] = [remote(piece, piece, c_s.at[t], c_r.at[t], cs[0])]

    def arrived(copies):
        for copy in copies:
            copy.wait_recv()
        sends.extend(copies)

    for t in range(n + 4):
        if t < n:
            issue_z(t)
        if t == 0:
            small_z = [
                remote(g_small.at[z, y], g_small.at[z, y], sm_s.at[k], sm_r.at[k], zs[k])
                for k in range(lay.nz - 1)
            ]
        if t == 1:
            arrived(small_z)
            small_y = [
                remote(
                    g_small.at[:, y], g_small.at[:, y],
                    sm_s.at[lay.nz - 1 + k], sm_r.at[lay.nz - 1 + k], ys[k],
                )
                for k in range(lay.ny - 1)
            ]
            halo_z[0].wait_recv()
            halo_z[1].wait_recv()
            halo_z[2].wait_recv()
            even = lax.rem(b, 2) == 0
            own = pltpu.make_async_remote_copy(
                src_ref=tok, dst_ref=tok_halo.at[1], send_sem=h_s.at[3], recv_sem=h_r.at[3],
                device_id=around[2], device_id_type=MESH,
            )
            passed = pltpu.make_async_remote_copy(
                src_ref=tok_halo.at[0], dst_ref=tok_halo.at[1], send_sem=h_s.at[3],
                recv_sem=h_r.at[3], device_id=around[3], device_id_type=MESH,
            )

            @pl.when(even)
            def _():
                own.start()

            @pl.when(jnp.logical_not(even))
            def _():
                passed.start()

        if 0 <= t - 1 < n:
            arrived(stage_z[t - 1])
            issue_1(t - 1)
        if 0 <= t - 2 < n:
            arrived(stage_1[t - 2])
            issue_2(t - 2)
        if 0 <= t - 3 < n:
            arrived(stage_2[t - 3])
            issue_c(t - 3)
        if 0 <= t - 4 < n:
            arrived(stage_c[t - 4])
    arrived(small_y)
    own.wait()
    for copy in sends:
        copy.wait_send()


def hbm(count):
    return [pl.BlockSpec(memory_space=pltpu.HBM)] * count


def dma(*shape):
    return pltpu.SemaphoreType.DMA(shape)


def gather(lay, u_att, u_up, u_down, small, tok, seg):
    r = u_att.shape[-2]
    n = len(CHUNKS)
    bf = jnp.bfloat16
    outs = (
        jax.ShapeDtypeStruct(block_shape(lay, 0, r), bf),
        jax.ShapeDtypeStruct(block_shape(lay, 1, r), bf),
        jax.ShapeDtypeStruct(block_shape(lay, 2, r), bf),
        jax.ShapeDtypeStruct((lay.nz, lay.ny) + small.shape, bf),
        jax.ShapeDtypeStruct((2,) + tok.shape, bf),
        jax.ShapeDtypeStruct((2,) + seg.shape, jnp.int32),
    )
    lx, ly, lz = max(1, lay.nx - 1), max(1, lay.ny - 1), max(1, lay.nz - 1)
    return pl.pallas_call(
        functools.partial(gather_kernel, lay),
        name="gather_weights",
        out_shape=outs,
        in_specs=hbm(6),
        out_specs=tuple(hbm(6)),
        scratch_shapes=[
            dma(4), dma(n, lz), dma(n, lz), dma(n, ly), dma(n, ly), dma(n, lx), dma(n, lx),
            dma(n), dma(n), dma(lz + ly), dma(lz + ly), dma(4), dma(4),
        ],
        compiler_params=pltpu.CompilerParams(collective_id=0, has_side_effects=True),
    )(u_att, u_up, u_down, small, tok, seg)


def reduce_kernel(
    lay, p_att, p_up, p_down, vec,
    f_att, f_up, f_down, vec_out,
    ca, ra1, rb1, ra2, rb2, ra3, v_c, v_x, v_y, v_z, *sems,
):
    (c_s, c_r, x_s, x_r, y_s, y_r, z_s, z_r, fx_s, fx_r, fc_s, fc_r, v_s, v_r) = sems
    x, c, z, y = lay.coords()
    xs, cs, zs, ys = line_peers(lay)
    barrier_with(xs + cs + zs + ys)
    ps = (p_att, p_up, p_down)
    fs = (f_att, f_up, f_down)
    n = len(CHUNKS)
    sends = []
    bf = jnp.bfloat16
    f32 = jnp.float32

    def arrived(copies):
        for copy in copies:
            copy.wait_recv()
        sends.extend(copies)

    v_c[c] = vec[...]
    vec_stage = [remote(v_c.at[c], v_c.at[c], v_s.at[0], v_r.at[0], cs[0])]
    arrived(vec_stage)
    v_x[x] = v_c[0] + v_c[1]
    vec_stage = [
        remote(v_x.at[x], v_x.at[x], v_s.at[1 + k], v_r.at[1 + k], p) for k, p in enumerate(xs)
    ]
    state = {"stage": vec_stage}

    def vec_step(step):
        if step == 0:
            arrived(state["stage"])
            v_y[y] = sum([v_x[k] for k in range(1, lay.nx)], v_x[0])
            at = lay.nx
            state["stage"] = [
                remote(v_y.at[y], v_y.at[y], v_s.at[at + k], v_r.at[at + k], p)
                for k, p in enumerate(ys)
            ]
        elif step == 1:
            arrived(state["stage"])
            v_z[z] = sum([v_y[k] for k in range(1, lay.ny)], v_y[0])
            at = lay.nx + lay.ny - 1
            state["stage"] = [
                remote(v_z.at[z], v_z.at[z], v_s.at[at + k], v_r.at[at + k], p)
                for k, p in enumerate(zs)
            ]
        elif step == 2:
            arrived(state["stage"])
            vec_out[...] = sum([v_z[k] for k in range(1, lay.nz)], v_z[0])

    def add_into(dst, srcs):
        lead = dst.shape[:-2]
        count = math.prod(lead)

        def body(j, carry):
            index = []
            rest = j
            for size in reversed(lead):
                index.append(lax.rem(rest, size))
                rest = rest // size
            index = tuple(reversed(index))
            total = dst[index].astype(f32)
            for src in srcs:
                total = total + src[index].astype(f32)
            dst[index] = total.astype(bf)
            return carry

        lax.fori_loop(0, count, body, 0)

    st_c, st_1, st_2, st_3, st_x, st_f = {}, {}, {}, {}, {}, {}

    def recv(bufs, t):
        g, i = CHUNKS[t]
        return bufs, g, i

    def buf(ref, g, i):
        return ref[g].at[i]

    def issue_core(t):
        g, i = CHUNKS[t]
        st_c[t] = [
            remote(
                view(lay, ps[g], g, i, 1 - c, ALL, ALL, ALL), buf(ca, g, i),
                c_s.at[t], c_r.at[t], cs[0],
            )
        ]

    def issue_1(t):
        g, i = CHUNKS[t]
        add_into(view(lay, ps[g], g, i, c, ALL, ALL, ALL), [buf(ca, g, i)])
        if i < 2:
            st_1[t] = [
                remote(
                    view(lay, ps[g], g, i, c, wrap(x + 1 + k, lay.nx), ALL, ALL),
                    buf(ra1, g, i).at[k], x_s.at[t, k], x_r.at[t, k], p,
                )
                for k, p in enumerate(xs)
            ]
        else:
            st_1[t] = [
                remote(
                    view(lay, ps[g], g, i, c, ALL, ALL, wrap(y + 1 + k, lay.ny)),
                    buf(rb1, g, 0).at[k], y_s.at[t, k], y_r.at[t, k], p,
                )
                for k, p in enumerate(ys)
            ]

    def issue_2(t):
        g, i = CHUNKS[t]
        if i < 2:
            add_into(
                view(lay, ps[g], g, i, c, x, ALL, ALL),
                [buf(ra1, g, i).at[k] for k in range(lay.nx - 1)],
            )
            st_2[t] = [
                remote(
                    view(lay, ps[g], g, i, c, x, ALL, wrap(y + 1 + k, lay.ny)),
                    buf(ra2, g, i).at[k], y_s.at[t, k], y_r.at[t, k], p,
                )
                for k, p in enumerate(ys)
            ]
        else:
            add_into(
                view(lay, ps[g], g, i, c, ALL, ALL, y),
                [buf(rb1, g, 0).at[k] for k in range(lay.ny - 1)],
            )
            st_2[t] = [
                remote(
                    view(lay, ps[g], g, i, c, wrap(x + 1 + k, lay.nx), ALL, y),
                    buf(rb2, g, 0).at[k], x_s.at[t, k], x_r.at[t, k], p,
                )
                for k, p in enumerate(xs)
            ]

    def issue_3(t):
        g, i = CHUNKS[t]
        second = (
            [buf(ra2, g, i).at[k] for k in range(lay.ny - 1)]
            if i < 2
            else [buf(rb2, g, 0).at[k] for k in range(lay.nx - 1)]
        )
        add_into(view(lay, ps[g], g, i, c, x, ALL, y), second)
        st_3[t] = [
            remote(
                view(lay, ps[g], g, i, c, x, wrap(z + 1 + k, lay.nz), y),
                buf(ra3, g, i).at[k], z_s.at[t, k], z_r.at[t, k], p,
            )
            for k, p in enumerate(zs)
        ]

    def final(ref, g, i, cc, xx):
        if g < 2:
            return ref.at[cc, xx, i]
        if isinstance(xx, slice):
            return ref.at[i, :, :, cc, :]
        return ref.at[i, lax.rem(xx, lay.sub), :, cc, xx // lay.sub]

    def issue_x(t):
        g, i = CHUNKS[t]
        own = view(lay, ps[g], g, i, c, x, z, y)
        srcs = [buf(ra3, g, i).at[k] for k in range(lay.nz - 1)]
        out = final(fs[g], g, i, c, x)
        for u in range(own.shape[0]):
            total = own[u].astype(f32)
            for src in srcs:
                total = total + src[u].astype(f32)
            out[u] = total.astype(bf)
        st_x[t] = [remote(out, out, fx_s.at[t, k], fx_r.at[t, k], p) for k, p in enumerate(xs)]

    def issue_f(t):
        g, i = CHUNKS[t]
        out = final(fs[g], g, i, c, ALL)
        st_f[t] = [remote(out, out, fc_s.at[t], fc_r.at[t], cs[0])]

    for t in range(n + 6):
        if t < n:
            issue_core(t)
        if 0 <= t - 1 < n:
            arrived(st_c[t - 1])
            issue_1(t - 1)
        if 0 <= t - 2 < n:
            arrived(st_1[t - 2])
            issue_2(t - 2)
        if 0 <= t - 3 < n:
            arrived(st_2[t - 3])
            issue_3(t - 3)
        if 0 <= t - 4 < n:
            arrived(st_3[t - 4])
            issue_x(t - 4)
        if 0 <= t - 5 < n:
            arrived(st_x[t - 5])
            issue_f(t - 5)
        if 0 <= t - 6 < n:
            arrived(st_f[t - 6])
        if 1 <= t <= 3:
            vec_step(t - 1)
    for copy in sends:
        copy.wait_send()


def final_shape(lay, group, r):
    if group < 2:
        return (2, lay.nx, 3, lay.unit, r, LANES)
    return (3, lay.sub, lay.down_unit, 2, lay.nx // lay.sub, r, LANES)


def reduce(lay, p_att, p_up, p_down, vec):
    r = p_att.shape[-2]
    n = len(CHUNKS)
    bf = jnp.bfloat16
    outs = tuple(jax.ShapeDtypeStruct(final_shape(lay, g, r), bf) for g in range(3)) + (
        jax.ShapeDtypeStruct(vec.shape, vec.dtype),
    )
    lx, ly, lz = max(1, lay.nx - 1), max(1, lay.ny - 1), max(1, lay.nz - 1)

    def bufs(chunks, peers, x_all, z_all, y_all):
        return [
            pltpu.VMEM((chunks,) + peers + part_shape(lay, g, x_all, z_all, y_all, r), bf)
            for g in range(3)
        ]

    scratch = [
        bufs(3, (), True, True, True),
        bufs(2, (lx,), False, True, True),
        bufs(1, (ly,), True, True, False),
        bufs(2, (ly,), False, True, False),
        bufs(1, (lx,), False, True, False),
        bufs(3, (lz,), False, False, False),
    ]
    vecs = [pltpu.VMEM((k,) + vec.shape, jnp.float32) for k in (2, lay.nx, lay.ny, lay.nz)]
    nv = 1 + lay.nx + lay.ny + lay.nz
    sems = [
        dma(n), dma(n), dma(n, lx), dma(n, lx), dma(n, ly), dma(n, ly), dma(n, lz), dma(n, lz),
        dma(n, lx), dma(n, lx), dma(n), dma(n), dma(nv), dma(nv),
    ]
    vmem = [pl.BlockSpec(memory_space=pltpu.VMEM)]
    return pl.pallas_call(
        functools.partial(reduce_kernel, lay),
        name="reduce_grads",
        out_shape=outs,
        in_specs=vmem * 4,
        out_specs=tuple(vmem * 4),
        scratch_shapes=scratch + vecs + sems,
        compiler_params=pltpu.CompilerParams(
            collective_id=1, has_side_effects=True, vmem_limit_bytes=VMEM_LIMIT
        ),
    )(p_att, p_up, p_down, vec)


NT = (((1,), (1,)), ((), ()))
NN = (((1,), (0,)), ((), ()))


def attention_kernel(rows, least_ref, qseg_ref, kseg_ref, q_ref, k_ref, v_ref, do_ref,
                     ctx_ref, dq_ref, dk_ref, dv_ref, bias, dk_acc, dv_acc):
    f32, bf = jnp.float32, jnp.bfloat16
    span = 3 * rows

    @pl.when(pl.program_id(0) == 0)
    def _():
        key_at = lax.broadcasted_iota(jnp.int32, (span, rows), 0)
        query_at = lax.broadcasted_iota(jnp.int32, (span, rows), 1) + 2 * rows
        allowed = (kseg_ref[...] == qseg_ref[...]) & (key_at <= query_at) & (key_at >= least_ref[0])
        bias[...] = jnp.where(allowed, 0.0, -1e30)

    tile = 256
    lane = lax.broadcasted_iota(jnp.int32, (tile, LANES), 1)
    v_t = v_ref[...].T
    k_t = k_ref[...].T
    do_t = do_ref[...].astype(f32).T
    dk_acc[...] = jnp.zeros_like(dk_acc)
    dv_acc[...] = jnp.zeros_like(dv_acc)
    for t in range(rows // tile):
        cols = slice(t * tile, (t + 1) * tile)
        kl = 2 * rows + (t + 1) * tile
        ctx_t, dq_t = [], []
        for hh in range(2):
            mine = (lane // HD) == hh
            zero = jnp.zeros((), bf)
            qm = jnp.where(mine, q_ref[cols, :], zero)
            dom = jnp.where(mine, do_ref[cols, :], zero)
            st = lax.dot_general(k_ref[:kl, :], qm, NT, preferred_element_type=f32)
            st = st + bias[:kl, cols]
            top = jnp.max(st, 0, keepdims=True)
            p = jnp.exp(st - top)
            w = p * (1.0 / jnp.sum(p, 0, keepdims=True))
            wb = w.astype(bf)
            half = slice(hh * HD, (hh + 1) * HD)
            o_t = lax.dot_general(v_t[half, :kl], wb, NN, preferred_element_type=f32)
            dp = lax.dot_general(v_ref[:kl, :], dom, NT, preferred_element_type=f32)
            delta = jnp.sum(o_t * do_t[half, cols], 0, keepdims=True)
            ds = (w * (dp - delta)).astype(bf)
            ctx_t.append(o_t)
            dq_t.append(lax.dot_general(k_t[half, :kl], ds, NN, preferred_element_type=f32))
            dk_acc[:kl, :] += lax.dot_general(ds, qm, NN, preferred_element_type=f32)
            dv_acc[:kl, :] += lax.dot_general(wb, dom, NN, preferred_element_type=f32)
        ctx_ref[cols, :] = jnp.concatenate(ctx_t, 0).T.astype(bf)
        dq_ref[cols, :] = jnp.concatenate(dq_t, 0).T
    dk_ref[...] = dk_acc[...]
    dv_ref[...] = dv_acc[...]


def attention(least, qseg, kseg, q, k, v, do):
    rows = q.shape[0]
    span = 3 * rows
    f32 = jnp.float32
    own = pl.BlockSpec((rows, LANES), lambda p: (0, p))
    wide = pl.BlockSpec((span, LANES), lambda p: (0, p))
    return pl.pallas_call(
        functools.partial(attention_kernel, rows),
        name="attention",
        grid=(PAIRS,),
        out_shape=(
            jax.ShapeDtypeStruct((rows, D), jnp.bfloat16),
            jax.ShapeDtypeStruct((rows, D), f32),
            jax.ShapeDtypeStruct((span, D), f32),
            jax.ShapeDtypeStruct((span, D), f32),
        ),
        in_specs=[
            pl.BlockSpec(memory_space=pltpu.SMEM),
            pl.BlockSpec((1, rows), lambda p: (0, 0)),
            pl.BlockSpec((span, 1), lambda p: (0, 0)),
            own, wide, wide, own,
        ],
        out_specs=(own, own, wide, wide),
        scratch_shapes=[
            pltpu.VMEM((span, rows), f32), pltpu.VMEM((span, LANES), f32), pltpu.VMEM((span, LANES), f32),
        ],
        compiler_params=pltpu.CompilerParams(vmem_limit_bytes=VMEM_LIMIT),
    )(least, qseg, kseg, q, k, v, do)


def norm_parts(values):
    middle = jnp.mean(values, -1, keepdims=True)
    centred = values - middle
    factor = lax.rsqrt(jnp.mean(centred * centred, -1, keepdims=True) + 1e-05)
    return centred * factor, factor


def norm_back(grad, gain, normed, factor):
    inner = grad * gain
    return factor * (
        inner
        - jnp.mean(inner, -1, keepdims=True)
        - normed * jnp.mean(inner * normed, -1, keepdims=True)
    )


def rotary_tables(positions):
    half = ROT // 2
    inverse = 10000.0 ** (-(2.0 * jnp.arange(half, dtype=jnp.float32)) / ROT)
    angles = positions.astype(jnp.float32)[:, None] * inverse[None, :]
    cosine = jnp.cos(angles)
    sine = jnp.sin(angles)
    return (jnp.concatenate([cosine, cosine], -1), jnp.concatenate([sine, sine], -1))


def rotate(values, cosine, sine):
    half = ROT // 2
    part = values[..., :ROT]
    turned = jnp.concatenate([-part[..., half:], part[..., :half]], -1)
    moved = part * cosine[:, None, :] + turned * sine[:, None, :]
    return jnp.concatenate([moved, values[..., ROT:]], -1)


def rotate_back(grad, cosine, sine):
    half = ROT // 2
    part = grad[..., :ROT]
    upper = part * sine[:, None, :]
    turned = jnp.concatenate([upper[..., half:], -upper[..., :half]], -1)
    moved = part * cosine[:, None, :] + turned
    return jnp.concatenate([moved, grad[..., ROT:]], -1)


def gelu_slope(pre):
    return 0.5 * (1.0 + lax.erf(pre / math.sqrt(2.0))) + pre * jnp.exp(
        -0.5 * pre * pre
    ) / math.sqrt(2.0 * math.pi)


def to_blocks(matrix, rows):
    return matrix.reshape(rows, -1, LANES).transpose(1, 0, 2)


def per_device(
    lay, tokens, seg_ids, out_grad, first_gain, first_bias, second_gain, second_bias,
    qkv_weight, qkv_bias, dense_weight, up_weight, up_bias, down_weight, out_bias,
):
    f32, bf = jnp.float32, jnp.bfloat16
    rows = tokens.shape[0]
    r = qkv_weight.shape[0]
    fsdp = lay.fsdp
    qkv_kinds = qkv_weight.reshape(r, H, 3, HD).transpose(0, 2, 1, 3).reshape(r, 3 * D)
    att_shape = block_shape(lay, 0, r)
    u_att = to_blocks(jnp.concatenate([qkv_kinds, dense_weight], 1), r)
    u_att = u_att.reshape(att_shape[:4] + att_shape[6:])
    u_up = to_blocks(up_weight, r).reshape(att_shape[:4] + att_shape[6:])
    down_shape = block_shape(lay, 2, r)
    u_down = (
        down_weight.reshape(4, r, PAIRS, LANES).transpose(2, 0, 1, 3)
        .reshape(down_shape[:3] + down_shape[5:])
    )
    vectors = (first_gain, first_bias, second_gain, second_bias, out_bias, qkv_bias, up_bias)
    sizes = [v.shape[0] for v in vectors]
    small = jnp.concatenate(vectors)
    small = jnp.pad(small, (0, 16 * LANES - small.shape[0])).reshape(16, LANES)
    seg_block = seg_ids.reshape(rows // LANES, LANES)
    g_att, g_up, g_down, g_small, tok_halo, seg_halo = gather(
        lay, u_att, u_up, u_down, small, tokens, seg_block
    )
    g_small = g_small.reshape(fsdp, 16 * LANES)
    full, at = [], 0
    for size in sizes:
        full.append(g_small[:, at : at + size].reshape(-1).astype(f32))
        at += size
    gain_first, shift_first, gain_second, shift_second, out_add, qkv_add, up_add = full
    att_mat = g_att.reshape(24, D, LANES).transpose(1, 0, 2).reshape(D, 4 * D)
    up_mat = g_up.reshape(24, D, LANES).transpose(1, 0, 2).reshape(D, FF)
    down_mat = g_down.reshape(PAIRS, FF, LANES).transpose(1, 0, 2).reshape(FF, D)
    q_mat, k_mat, v_mat, dense_mat = (att_mat[:, k * D : (k + 1) * D] for k in range(4))
    q_add, k_add, v_add = (qkv_add.reshape(H, 3, HD)[:, k].reshape(D) for k in range(3))

    block = lax.axis_index(("dp", "fsdp"))
    stream = tokens.astype(f32)
    tok_all = jnp.concatenate([tok_halo[0], tok_halo[1], tokens], 0).astype(f32)
    normed_all, factor_all = norm_parts(tok_all)
    first_all = (normed_all * gain_first + shift_first).astype(bf)
    normed, factor = normed_all[2 * rows :], factor_all[2 * rows :]
    first_in = first_all[2 * rows :]
    second_in = (normed * gain_second + shift_second).astype(bf)

    def mm(a, b):
        return jnp.dot(a, b, preferred_element_type=f32)

    key_pos = (block - 2) * rows + jnp.arange(3 * rows, dtype=jnp.int32)
    cosine, sine = rotary_tables((key_pos + ROW) % ROW)
    own_cos, own_sin = cosine[2 * rows :], sine[2 * rows :]
    scale = 1.0 / math.sqrt(HD)
    q_proj = (mm(first_in, q_mat) + q_add).reshape(rows, H, HD)
    query = (rotate(q_proj, own_cos, own_sin) * scale).astype(bf).reshape(rows, D)
    k_proj = (mm(first_all, k_mat) + k_add).reshape(3 * rows, H, HD)
    key = rotate(k_proj, cosine, sine).astype(bf).reshape(3 * rows, D)
    value = (mm(first_all, v_mat) + v_add).astype(bf)
    context_grad = lax.dot_general(out_grad, dense_mat, NT, preferred_element_type=f32).astype(bf)
    seg_all = jnp.concatenate([seg_halo[0], seg_halo[1], seg_block], 0).reshape(3 * rows, 1)
    least = jnp.maximum(0, 2 * rows - block * rows).astype(jnp.int32).reshape(1)
    context, dq, dk, dv = attention(
        least, seg_ids.reshape(1, rows), seg_all, query, key, value, context_grad
    )
    pre = mm(second_in, up_mat) + up_add
    activation = jax.nn.gelu(pre, approximate=False).astype(bf)
    result = stream + mm(context, dense_mat) + mm(activation, down_mat) + out_add
    output = result.astype(bf)

    cotangent = out_grad.astype(f32)
    down_grad = mm(activation.T, out_grad)
    dense_grad = mm(context.T, out_grad)
    hidden_grad = lax.dot_general(out_grad, down_mat, NT, preferred_element_type=f32)
    pre_grad = (hidden_grad * gelu_slope(pre)).astype(bf)
    up_grad = mm(second_in.T, pre_grad)
    second_grad = lax.dot_general(pre_grad, up_mat, NT, preferred_element_type=f32)
    dq = rotate_back((dq * scale).reshape(rows, H, HD), own_cos, own_sin).reshape(rows, D).astype(bf)
    dk = rotate_back(dk.reshape(3 * rows, H, HD), cosine, sine).reshape(3 * rows, D).astype(bf)
    dv = dv.astype(bf)
    q_grad = mm(first_in.T, dq)
    k_grad = mm(first_all.T, dk)
    v_grad = mm(first_all.T, dv)
    first_grad_all = lax.dot_general(dk, k_mat, NT, preferred_element_type=f32) + lax.dot_general(
        dv, v_mat, NT, preferred_element_type=f32
    )
    first_grad = first_grad_all[2 * rows :] + lax.dot_general(
        dq, q_mat, NT, preferred_element_type=f32
    )
    devices = lay.dp * fsdp
    for distance in (2, 1):
        low = (2 - distance) * rows
        route = [(i, (i - distance) % devices) for i in range(devices)]
        first_grad = first_grad + lax.ppermute(
            first_grad_all[low : low + rows].astype(bf), ("dp", "fsdp"), route
        ).astype(f32)
    input_grad = (
        cotangent
        + norm_back(first_grad, gain_first, normed, factor)
        + norm_back(second_grad, gain_second, normed, factor)
    ).astype(bf)

    docs = DOC_DEV * devices
    token_norm = (
        jnp.sum(jnp.square(activation.astype(f32)), -1) * jnp.sum(cotangent * cotangent, -1) / (FF * D)
    )
    member = (seg_ids[:, None] == jnp.arange(docs, dtype=jnp.int32)[None, :]).astype(f32)
    doc_sums = jnp.sum(token_norm[:, None] * member, 0)
    doc_counts = jnp.sum(member, 0)
    qkv_bias_grad = jnp.stack(
        [jnp.sum(v.astype(f32), 0).reshape(H, HD) for v in (dq, dk, dv)], 1
    ).reshape(3 * D)
    grads = (
        jnp.sum(first_grad * normed, 0),
        jnp.sum(first_grad, 0),
        jnp.sum(second_grad * normed, 0),
        jnp.sum(second_grad, 0),
        jnp.sum(cotangent, 0),
        qkv_bias_grad,
        jnp.sum(pre_grad.astype(f32), 0),
    )
    vec = jnp.concatenate(grads + (doc_sums, doc_counts))
    count = vec.shape[0]
    vec_rows = -(-count // (8 * LANES)) * 8
    vec = jnp.pad(vec, (0, vec_rows * LANES - count)).reshape(vec_rows, LANES)

    def blocks(matrix, shape):
        return matrix.astype(bf).reshape(matrix.shape[0], -1, LANES).transpose(1, 0, 2).reshape(shape)

    p_att = blocks(jnp.concatenate([q_grad, k_grad, v_grad, dense_grad], 1), att_shape)
    p_up = blocks(up_grad, att_shape)
    p_down = blocks(down_grad, down_shape)
    f_att, f_up, f_down, vec = reduce(lay, p_att, p_up, p_down, vec)
    vec = vec.reshape(-1)
    shard = lax.axis_index("fsdp")
    pieces, at = [], 0
    for size in sizes:
        pieces.append(lax.dynamic_slice_in_dim(vec, at + shard * size, size))
        at += size * fsdp
    totals, counts = vec[at : at + docs], vec[at + docs : at + 2 * docs]
    f_att = f_att.reshape(24, r, LANES).transpose(1, 0, 2).reshape(r, 4 * D).astype(f32)
    qkv_out = f_att[:, : 3 * D].reshape(r, 3, H, HD).transpose(0, 2, 1, 3).reshape(r, 3 * D)
    up_out = f_up.reshape(24, r, LANES).transpose(1, 0, 2).reshape(r, FF).astype(f32)
    down_out = (
        f_down.reshape(PAIRS, 4, r, LANES).transpose(1, 2, 0, 3).reshape(4 * r, D).astype(f32)
    )
    return (
        output,
        input_grad,
        pieces[0],
        pieces[1],
        pieces[2],
        pieces[3],
        qkv_out,
        pieces[5],
        f_att[:, 3 * D :],
        up_out,
        pieces[6],
        down_out,
        pieces[4],
        totals / counts,
    )


def solution(mesh):
    lay = Layout(mesh.shape["dp"], mesh.shape["fsdp"])
    both = P(("dp", "fsdp"))
    split = P("fsdp")
    in_specs = (both, both, both) + (split,) * 11
    out_specs = (both, both) + (split,) * 11 + (P(),)
    return jax.shard_map(
        functools.partial(per_device, lay), mesh=mesh, in_specs=in_specs, out_specs=out_specs,
        check_vma=False,
    )
```

time: 1200 us -> 491 us (0.41)
  waiting for transfers between devices: 636 us -> 0.01 us
  Pallas kernels: 0 us -> 281 us
  matrix products: 260 us -> 83.8 us
  blocking collectives: 169 us -> 0 us
  local copies, waits for them, and re-layouts: 42 us -> 83.9 us
  starting transfers between devices: 31.8 us -> 1.17 us
  between operations: 18 us -> 1.53 us
    reduce_scatter x4 -> x0, waiting for transfers between devices: 380 us -> none  [the longest x1 167 us: per_device(): lax.psum_scatter(up_weight_grad, 'fsdp', scatter_dimension=0, tiled=True)]
    pallas_call x0 -> x3, Pallas kernels: none -> 281 us  [the longest x1 125 us: gather(): pl.pallas_call(functools.partial(gather_kernel, lay), name='gather_weight...]
    ppermute x10 -> x2, waiting for transfers between devices: 192 us -> 0.01 us  [per_device(): lax.ppermute(first_grad_all[low:low + rows].astype(bf), ('dp', 'fsdp'), r...]
    dot_general x97 -> x18, matrix products: 260 us -> 83.8 us  [the longest x12 62.5 us: mm(): return jnp.dot(a, b, preferred_element_type=f32)]
    all_gather x4 -> x0, waiting for transfers between devices: 61.3 us -> none  [the longest x1 61.3 us: per_device(): lax.all_gather(qkv_weight, 'fsdp', axis=0, tiled=True)]
    unnamed x2 -> x0, blocking collectives: 60.2 us -> none
    all_gather x1 -> x0, blocking collectives: 57.8 us -> none  [per_device(): lax.all_gather(up_bias, 'fsdp', axis=0, tiled=True)]
    psum x2 -> x0, blocking collectives: 50.9 us -> none  [the longest x1 43.2 us: per_device(): totals = lax.psum((doc_sums, doc_counts), ('dp', 'fsdp'))]
  transfers between devices with their start and end apart: 19 -> 2, of which waited for: 10 -> 0; matrix products, arithmetic and copies ran while one was open for 27% -> 19% of each run, Pallas kernels for 0% -> 0%
where the time goes in v1:
time: 491 us; the launch traced here: 486 us
  Pallas kernels  281 us (57%)
  local copies, waits for them, and re-layouts  83.9 us (17%)
  matrix products  83.8 us (17%)
  other arithmetic  34.4 us (7%)
    pallas_call x1, Pallas kernels, gather(): pl.pallas_call(functools.partial(gather_kernel, lay), name='gather_weight...  125 us
    pallas_call x1, Pallas kernels, reduce(): pl.pallas_call(functools.partial(reduce_kernel, lay), name='reduce_grads'...  101 us
    dot_general x12, matrix products, mm(): return jnp.dot(a, b, preferred_element_type=f32)  62.5 us
    pallas_call x1, Pallas kernels, attention(): pl.pallas_call(functools.partial(attention_kernel, rows), name='attention...  54.6 us
    unnamed x90, local copies, waits for them, and re-layouts  11.4 us
    reshape x2, local copies, waits for them, and re-layouts, blocks(): matrix.astype(bf).reshape(matrix.shape[0], -1, LANES).transpose(1, 0, 2)  10.2 us
  transfers between devices with their start and end apart: 2, of which 0 were waited for; matrix products, arithmetic and copies ran while one was open for 19% of the time, Pallas kernels for 0%

profile of v1, /device:TPU:1, one launch (start us, length us, event | category | flops | bytes accessed | tf_op | source)
XLA Modules:
  0.0 486.0 jit_solution(5749408293681134660)
XLA Ops:
  1.6 4.8 concatenate.56
  13.2 125.5 %gather_weights.1 = (bf16[2,2,3,2,4,2,96,128]{7,6,5,4,3,2,1,0:T(8,128)(2,1)}, bf16[2,2,3,2,4,2,96,128]{7,6,5,4,3,2,1,0:T(8,128)(2,1)}, bf16[3,1,2,4,2,2,2,96,128...) custom-call(bf16[2,2,3,2,96,128]{5,4,3,2,1,0:T(8,128)(2,1)} %bitcast, ...), custom_call_target="tpu_custom_call" | custom-call | tf_op jit(solution)/shard_map/gather_weights/pallas_call | solution.py:260
  140.6 1.5 slice_bitcast_fusion.1
  142.5 3.9 fusion.18
  146.4 6.7 %copy.82 = bf16[24,768,128]{1,2,0:T(8,128)(2,1)} copy(bf16[24,768,128]{2,1,0:T(8,128)(2,1)} %bitcast.195) | data formatting | bytes 9437184 | tf_op jit(solution)/shard_map/reshape | solution.py:691
  153.2 4.3 add_convert_fusion.1
  157.5 1.4 copy-done.8
  158.9 3.3 convolution_add_fusion.2
  162.1 1.9 copy.83
  164.9 4.0 convolution_add_fusion.1
  171.5 1.4 slice.316
  174.2 3.2 fusion.31.do_ref
  179.7 5.7 %add_convert_fusion.v_ref = bf16[1536,768]{1,0:T(8,128)(2,1)} fusion(bf16[1536,768]{1,0:T(8,128)(2,1)} %copy-done.8, f32[768]{0:T(1024)S(1)} %add.209, bf16[768,3072]{0,1:T(8,128)(2,1)} %bitcast.166), kind=kOutput, calls=%fused_computation.40 | convolution fusion | flops 1814298624 | bytes 5901312 | tf_op jit(solution)/shard_map/dot_general | solution.py:707
  185.4 1.5 fusion.33
  187.1 2.5 copy.87.k_ref
  189.6 54.6 %attention.1 = (bf16[512,768]{1,0:T(8,128)(2,1)}, f32[512,768]{1,0:T(8,128)}, f32[1536,768]{1,0:T(8,128)}, f32[1536,768]{1,0:T(8,128)}) custom-call(s32[1]{0:T(128)} %bitcast.least_ref, s32[1,512]{1,0:T(1,128)} %bitcast.226, s32[1536,1]{1,0:T(8,128)} %bitcast.207, bf16[512,768]{1,0:T(8,128)(2,1)} %copy.86.q_ref, bf16[1536,768]{1,0:T(8,128)(2,1)} %copy.87.k_ref, ...), custom_call_target="tpu_custom_call" | custom-call | tf_op jit(solution)/shard_map/attention/pallas_call | solution.py:583
  244.2 6.2 %copy.90 = f32[1536,768]{0,1:T(8,128)} copy(f32[1536,768]{1,0:T(8,128)} %get-tuple-element.35) | data formatting | bytes 9437184 | tf_op jit(solution)/shard_map/attention/pallas_call | solution.py:583
  250.4 1.4 slice_multiply_fusion.1
  251.8 2.2 slice.224
  254.1 1.6 maximum_add_fusion
  256.7 2.1 fusion.38
  259.1 4.3 fusion.59
  266.8 3.2 convolution_convert_fusion.4
  270.1 1.6 copy.91
  272.8 1.4 slice.229
  274.4 6.7 %copy.88 = bf16[24,768,128]{1,2,0:T(8,128)(2,1)} copy(bf16[24,768,128]{2,1,0:T(8,128)(2,1)} %bitcast.186) | data formatting | bytes 9437184 | tf_op jit(solution)/shard_map/reshape | solution.py:692
  281.1 6.8 %copy.89 = bf16[6,3072,128]{1,2,0:T(8,128)(2,1)} copy(bf16[6,3072,128]{2,1,0:T(8,128)(2,1)} %bitcast.185) | data formatting | bytes 9437184 | tf_op jit(solution)/shard_map/reshape | solution.py:693
  288.0 4.9 fusion.28
  292.9 1.8 convolution_convert_fusion.2
  294.7 1.7 copy.95
  296.4 2.4 copy.94
  300.2 3.1 convolution_convert_fusion.3
  303.4 18.9 %multiply_reduce_fusion = (f32[512]{0:T(512)S(1)}, bf16[512,3072]{1,0:T(8,128)(2,1)S(1)}, f32[512,3072]{1,0:T(8,128)S(1)}) fusion(f32[3072]{0:T(1024)S(1)} %reshape.348, bf16[768,3072]{0,1:T(8,128)(2,1)} %bitcast.187, f32[1536,768]{1,0:T(8,128)} %get-tuple-element.96, f32[768]{0:T(1024)S(1)} %reshape.347, f32[768]{0:T(1024)S(1)} %reshape.346), kind=kOutput, calls=%fused_computation.11 | convolution fusion | flops 2525625856 | bytes 15749120 | tf_op jit(solution)/shard_map/dot_general | solution.py:707
  322.3 4.4 convolution_convert_fusion
  326.7 3.9 fusion.60
  330.6 5.2 %convert_reduce_fusion = (f32[3072]{0:T(1024)S(1)}, bf16[512,3072]{1,0:T(8,128)(2,1)S(1)}) fusion(f32[512,3072]{1,0:T(8,128)S(1)} %get-tuple-element.122, f32[3072]{0:T(1024)S(1)} %reshape.348, bf16[512,768]{1,0:T(8,128)(2,1)S(1)} %copy-done.14, bf16[3072,768]{0,1:T(8,128)(2,1)S(1)} %bitcast.194), kind=kOutput, calls=%fused_computation.12 | convolution fusion | flops 2436363264 | bytes 14966784 | tf_op jit(solution)/shard_map/dot_general | solution.py:732
  335.8 5.5 %fusion.21 = bf16[96,24,8,128]{3,2,1,0:T(8,128)(2,1)S(1)} fusion(bf16[512,3072]{1,0:T(8,128)(2,1)S(1)} %get-tuple-element.127, f32[1536,768]{1,0:T(8,128)} %get-tuple-element.96, f32[768]{0:T(1024)S(1)} %reshape.347, f32[768]{0:T(1024)S(1)} %reshape.346), kind=kOutput, calls=%fused_computation.52 | convolution fusion | flops 2419458048 | bytes 9443328 | tf_op jit(solution)/shard_map/dot_general | solution.py:707
  341.3 3.5 copy.125
  344.8 6.7 %copy.97 = bf16[3072,6,128]{2,0,1:T(8,128)(2,1)} copy(bf16[3072,6,128]{0,2,1:T(8,128)(2,1)} %bitcast.196) | data formatting | bytes 9437184 | tf_op jit(solution)/shard_map/reshape | solution.py:786
  351.5 3.9 add_convert_fusion.2
  355.4 5.0 %pad_maximum_fusion = bf16[768,24,128]{2,0,1:T(8,128)(2,1)} fusion(bf16[768,6,128]{2,0,1:T(8,128)(2,1)S(1)} %copy.95, bf16[768,6,128]{2,0,1:T(8,128)(2,1)} %copy.94, bf16[768,6,128]{2,0,1:T(8,128)(2,1)} %fusion.28, bf16[768,6,128]{2,0,1:T(8,128)(2,1)} %convolution_convert_fusion.3), kind=kLoop, calls=%fused_computation.37 | loop fusion | flops 7077888 | bytes 9437184 | tf_op jit(solution)/shard_map/concatenate | solution.py:788
  360.4 3.3 fusion.26
  363.8 3.3 multiply_reduce_fusion.1
  367.2 2.2 fusion.24
  370.2 101.2 %reduce_grads.1 = (bf16[2,2,3,2,96,128]{5,4,3,2,1,0:T(8,128)(2,1)}, bf16[2,2,3,2,96,128]{5,4,3,2,1,0:T(8,128)(2,1)}, bf16[3,1,2,2,2,96,128]{6,5,4,3,2,1,0:T(8,128)(2,1)}, f32[80,128]{1,0:T(8,128)}) custom-call(bf16[2,2,3,2,4,2,96,128]{7,6,5,4,3,2,1,0:T(8,128)(2,1)} %bitcast.157, bf16[2,2,3,2,4,2,96,128]{7,6,5,4,3,2,1,0:T(8,128)(2,1)} %bitcast.155, ...), custom_call_target="tpu_custom_call" | custom-call | tf_op jit(solution)/shard_map/reduce_grads/pallas_call | solution.py:511
  479.6 2.2 copy_bitcast_fusion.2
  481.8 1.4 copy.102
  484.4 1.4 fusion.58
  (167 shorter events, 35.1 us)
Async XLA Ops:
  0.6 10.1 %copy-start = (bf16[96,3072]{1,0:T(8,128)(2,1)S(1)}, bf16[96,3072]{1,0:T(8,128)(2,1)}, u32[]{:S(2)}) copy-start(bf16[96,3072]{1,0:T(8,128)(2,1)} %param.24) | copy-start | bytes 1769476
  0.7 11.0 %copy-start.16 = (bf16[384,768]{1,0:T(8,128)(2,1)S(1)}, bf16[384,768]{1,0:T(8,128)(2,1)}, u32[]{:S(2)}) copy-start(bf16[384,768]{1,0:T(8,128)(2,1)} %param.26) | copy-start | bytes 1769476
  10.7 131.4 %copy-start.2 = (bf16[512,768]{1,0:T(8,128)(2,1)S(1)}, bf16[512,768]{1,0:T(8,128)(2,1)}, u32[]{:S(2)}) copy-start(bf16[512,768]{1,0:T(8,128)(2,1)} %tok.1) | copy-start | bytes 2359300
  139.5 13.7 %copy-start.19 = (bf16[1,8,16,128]{3,1,2,0:T(8,128)(2,1)}, bf16[1,8,16,128]{3,1,2,0:T(8,128)(2,1)S(1)}, u32[]{:S(2)}) copy-start(bf16[1,8,16,128]{3,1,2,0:T(8,128)(2,1)S(1)} %copy.127) | copy-start | bytes 98308
  140.5 12.6 %copy-start.21 = (f32[768]{0:T(1024)}, f32[768]{0:T(1024)S(1)}, u32[]{:S(2)}) copy-start(f32[768]{0:T(1024)S(1)} %reshape.343) | copy-start | bytes 9220
  146.4 120.1 %copy-start.20 = (f32[1536]{0:T(1024)}, f32[1536]{0:T(1024)S(1)}, u32[]{:S(2)}) copy-start(f32[1536]{0:T(1024)S(1)} %add_rsqrt_fusion) | copy-start | bytes 18436
  157.5 1.4 copy-start.8
  168.9 2.6 copy-start.5
  168.9 4.0 copy-start.27
  168.9 4.0 copy-start.23
  179.7 5.7 %copy-start.10 = (f32[1536,12,8]{0,2,1:T(8,128)S(1)}, f32[1536,12,8]{0,2,1:T(8,128)}, u32[]{:S(2)}) copy-start(f32[1536,12,8]{0,2,1:T(8,128)} %get-tuple-element.93) | copy-start | bytes 1769476
  179.7 5.7 %copy-start.11 = (f32[1536,12,8]{0,2,1:T(8,128)S(1)}, f32[1536,12,8]{0,2,1:T(8,128)}, u32[]{:S(2)}) copy-start(f32[1536,12,8]{0,2,1:T(8,128)} %get-tuple-element.94) | copy-start | bytes 1769476
  179.7 7.2 %copy-start.4 = (bf16[1536,12,48]{0,2,1:T(8,128)(2,1)S(1)}, bf16[1536,12,48]{0,2,1:T(8,128)(2,1)}, u32[]{:S(2)}) copy-start(bf16[1536,12,48]{0,2,1:T(8,128)(2,1)} %slice.316) | copy-start | bytes 5308420
  254.0 2.5 slice-start.2
  254.1 2.6 slice-start.3
  255.8 3.3 slice-start
  256.2 2.5 copy-start.6
  256.7 2.4 slice-start.1
  263.4 3.5 copy-start.9
  264.6 95.8 %collective-permute-start = (bf16[512,768]{1,0:T(8,128)(2,1)}, bf16[512,768]{1,0:T(8,128)(2,1)}, u32[]{:S(2)}, u32[]{:S(2)}) collective-permute-start(bf16[512,768]{1,0:T(8,128)(2,1)} %get-tuple-element.97), channel_id=1, source_target_pairs={{0,30},{1,31},{2,0},{3,1},{4,2},{5,3},{6,4},{7,5},{8,6},{9,7},{10,... | collective-permute-start | bytes 2359304 | tf_op jit(solution)/shard_map/ppermute | solution.py:752
  265.6 94.8 %collective-permute-start.1 = (bf16[512,768]{1,0:T(8,128)(2,1)}, bf16[512,768]{1,0:T(8,128)(2,1)}, u32[]{:S(2)}, u32[]{:S(2)}) collective-permute-start(bf16[512,768]{1,0:T(8,128)(2,1)} %get-tuple-element.98), channel_id=1, source_target_pairs={{0,31},{1,0},{2,1},{3,2},{4,3},{5,4},{6,5},{7,6},{8,7},{9,8},{10,9... | collective-permute-start | bytes 2359304 | tf_op jit(solution)/shard_map/ppermute | solution.py:752
  266.8 3.2 copy-start.12
  270.0 1.7 copy-start.18
  270.0 4.2 copy-start.26
  270.0 4.2 copy-start.25
  281.1 6.9 %copy-start.7 = (bf16[1536,12,64]{0,2,1:T(8,128)(2,1)S(1)}, bf16[1536,12,64]{0,2,1:T(8,128)(2,1)}, u32[]{:S(2)}) copy-start(bf16[1536,12,64]{0,2,1:T(8,128)(2,1)} %copy-done.6) | copy-start | bytes 7077892
  288.0 4.9 %copy-start.13 = (bf16[512,768]{1,0:T(8,128)(2,1)S(1)}, bf16[512,768]{1,0:T(8,128)(2,1)}, u32[]{:S(2)}) copy-start(bf16[512,768]{1,0:T(8,128)(2,1)} %param.16) | copy-start | bytes 2359300
  288.0 4.9 %copy-start.28 = (bf16[512,768]{1,0:T(8,128)(2,1)S(1)}, bf16[512,768]{1,0:T(8,128)(2,1)}, u32[]{:S(2)}) copy-start(bf16[512,768]{1,0:T(8,128)(2,1)} %get-tuple-element.32) | copy-start | bytes 2359300
  292.9 6.0 %copy-start.17 = (f32[512,16]{0,1:T(8,128)S(1)}, f32[512,16]{0,1:T(8,128)}, u32[]{:S(2)}) copy-start(f32[512,16]{0,1:T(8,128)} %get-tuple-element.131) | copy-start | bytes 98308
  300.2 26.5 %slice-start.8 = ((s8[4718592]{0:T(1024)(128)(4,1)}), s8[4194304]{0:T(1024)(128)(4,1)S(1)}, s32[]{:S(2)}) async-start(s8[4718592]{0:T(1024)(128)(4,1)} %bitcast.191), calls=%async_computation.8 | async-start | bytes 8388608
  303.3 19.0 %copy-start.14 = (bf16[512,768]{1,0:T(8,128)(2,1)S(1)}, bf16[512,768]{1,0:T(8,128)(2,1)}, u32[]{:S(2)}) copy-start(bf16[512,768]{1,0:T(8,128)(2,1)} %param.16) | copy-start | bytes 2359300
  303.3 23.3 %slice-start.9 = ((s8[4718592]{0:T(1024)(128)(4,1)}), s8[524288]{0:T(1024)(128)(4,1)S(1)}, s32[]{:S(2)}) async-start(s8[4718592]{0:T(1024)(128)(4,1)} %bitcast.191), calls=%async_computation.9 | async-start | bytes 1048576
  335.8 5.5 %copy-start.29 = (bf16[512,3072]{1,0:T(8,128)(2,1)}, bf16[512,3072]{1,0:T(8,128)(2,1)S(1)}, u32[]{:S(2)}) copy-start(bf16[512,3072]{1,0:T(8,128)(2,1)S(1)} %get-tuple-element.127) | copy-start | bytes 9437188
  344.8 6.7 %copy-start.3 = (bf16[512,768]{1,0:T(8,128)(2,1)S(1)}, bf16[512,768]{1,0:T(8,128)(2,1)}, u32[]{:S(2)}) copy-start(bf16[512,768]{1,0:T(8,128)(2,1)} %tok.1) | copy-start | bytes 2359300
  351.5 12.2 %slice-start.4 = ((s8[4718592]{0:T(1024)(128)(4,1)}), s8[4194304]{0:T(1024)(128)(4,1)S(1)}, s32[]{:S(2)}) async-start(s8[4718592]{0:T(1024)(128)(4,1)} %bitcast.174), calls=%async_computation.4 | async-start | bytes 8388608
  351.5 12.2 %slice-start.6 = ((s8[4718592]{0:T(1024)(128)(4,1)}), s8[4194304]{0:T(1024)(128)(4,1)S(1)}, s32[]{:S(2)}) async-start(s8[4718592]{0:T(1024)(128)(4,1)} %bitcast.188), calls=%async_computation.6 | async-start | bytes 8388608
  355.4 8.4 %slice-start.5 = ((s8[4718592]{0:T(1024)(128)(4,1)}), s8[524288]{0:T(1024)(128)(4,1)S(1)}, s32[]{:S(2)}) async-start(s8[4718592]{0:T(1024)(128)(4,1)} %bitcast.174), calls=%async_computation.5 | async-start | bytes 1048576
  355.4 8.4 %slice-start.7 = ((s8[4718592]{0:T(1024)(128)(4,1)}), s8[524288]{0:T(1024)(128)(4,1)S(1)}, s32[]{:S(2)}) async-start(s8[4718592]{0:T(1024)(128)(4,1)} %bitcast.188), calls=%async_computation.7 | async-start | bytes 1048576
  360.4 3.3 copy-start.22
  360.4 3.3 copy-start.30
  363.8 3.4 copy-start.15
  363.8 3.4 slice-start.10
  367.1 2.3 copy-start.24
  478.2 7.7 %copy-start.1 = (bf16[96,3072]{1,0:T(8,128)(2,1)S(1)}, bf16[96,3072]{1,0:T(8,128)(2,1)}, u32[]{:S(2)}) copy-start(bf16[96,3072]{1,0:T(8,128)(2,1)} %param.24) | copy-start | bytes 1769476
